TPU v7x, 32 devices: a whole 2x2x4 slice. The times are simulated.
32 devices in a mesh: chi: 4 (over y, x), dl: 4 (over z), cell: 2 (over core).
Axes of the slice: x: 2, y: 2, z: 4, core: 2. Of those that a mesh axis runs over, the one named last changes fastest.
Arguments:
- left_env: bfloat16 [2, 512, 512, 36], P('cell', None, 'chi'), may hold values from -6 to 6
- up_left: bfloat16 [2, 512, 36, 512], P('cell', 'chi', None, 'dl'), may hold values from -0.109375 to 0.109375
- up_center: bfloat16 [2, 512, 36, 512], P('cell', 'chi', None, 'dl'), may hold values from -0.109375 to 0.109375
- right_env: bfloat16 [2, 512, 36, 512], P('cell', 'dl'), may hold values from -0.046875 to 0.046875
- center: bfloat16 [2, 512, 512], P('cell', None, 'dl'), may hold values from -0.25 to 0.25
- ket_tensor: bfloat16 [2, 6, 6, 6, 6, 2], P('cell'), may hold values from -0.875 to 0.875
Outputs:
- left_env_new: float32 [2, 512, 36, 512], P('cell', 'chi', None, 'dl')
- new_left: float32 [2, 512, 36, 512], P('cell', 'chi', None, 'dl')
All inputs are finite; a program needn't handle non-finite values.
Results may differ from a plain program's by a relative error of at most 0.0066.
The roundings to bfloat16 on the way count: a program that leaves them out, or rounds other values in their place, can miss the bound.
Values may be sent and summed in bfloat16 or wider, within the bound.
A program may use at most 256 MiB of HBM per device.

v0:
```python
import math
import jax
import jax.numpy as jnp
from jax import lax
from jax.experimental.layout import Layout, with_layout_constraint
from jax.sharding import PartitionSpec as P

ITERS = 5
HIGH = lax.Precision.HIGH
F32 = jnp.float32
BF16 = jnp.bfloat16


def from_behind(block, axis, distance):
    devices = range(lax.axis_size(axis))
    route = [((i - distance) % len(devices), i) for i in devices]
    return lax.ppermute(block, axis, route)


def pick(rows, cols, row_of, col_of):
    r = lax.broadcasted_iota(jnp.int32, (rows, cols), 0)
    c = lax.broadcasted_iota(jnp.int32, (rows, cols), 1)
    return (row_of(r) == col_of(c)).astype(BF16)


def double_layer(tensor, pad):
    leg = tensor.shape[0]
    two = leg * leg
    phys = tensor.shape[4]
    big = two * pad

    def outer(first):

        def code(n):
            m, s = (n // pad, n % pad)
            a = m // leg if first else m % leg
            b = s // leg if first else s % leg
            return jnp.where(s < two, a * leg + b, -1)

        return code

    def same(n):
        return n

    total = None
    ket_rows = pick(big, two, outer(True), same)
    bra_rows = pick(big, two, outer(False), same)
    for p in range(phys):
        mat = tensor[:, :, :, :, p].reshape(two, two)
        ket_small = jnp.dot(ket_rows, mat, preferred_element_type=F32).astype(BF16)
        bra_small = jnp.dot(bra_rows, mat, preferred_element_type=F32).astype(BF16)
        ket = lax.dot_general(
            ket_small, ket_rows, (((1,), (1,)), ((), ())), preferred_element_type=F32
        )
        bra = lax.dot_general(
            bra_small, bra_rows, (((1,), (1,)), ((), ())), preferred_element_type=F32
        )
        total = ket * bra if total is None else total + ket * bra
    return total.astype(BF16)


def row_major(block):
    return with_layout_constraint(block, Layout(major_to_minor=tuple(range(block.ndim))))


def site_input(env, stacked):
    summed = jnp.einsum("abm,csa->cmsb", env, stacked, preferred_element_type=F32).astype(BF16)
    summed = row_major(summed)
    columns, two, pad, amount = summed.shape
    return summed.reshape(columns, two * pad, amount)


def site_output(flat, layer, pad):
    out = jnp.einsum("tn,ctb->cnb", layer, flat, preferred_element_type=F32).astype(BF16)
    return out.reshape(out.shape[0], out.shape[1] // pad, pad, out.shape[2])


def spread_rows(block, pad):
    turned = jnp.pad(block.transpose(2, 1, 0), ((0, 0), (0, pad - block.shape[1]), (0, 0)))
    return lax.all_gather(row_major(turned), "chi", axis=2, tiled=True)


def shards(left_env, up_left, up_center, right_env, center, ket_tensor):
    env_local = left_env[0]
    left_iso = up_left[0]
    left_mid = up_center[0]
    env_right = right_env[0]
    bond_mat = center[0]
    site_ket = ket_tensor[0]
    chi_all = env_local.shape[0]
    leg_width = env_local.shape[2]
    pad = -(-leg_width // 8) * 8
    rows = left_iso.shape[0]
    col_count = left_iso.shape[2]
    mid_all = spread_rows(left_mid, pad)
    iso_all = spread_rows(left_iso, pad)
    next_iso = from_behind(left_iso, "cell", -1)
    bra_iso = lax.all_gather(next_iso, "dl", axis=2, tiled=True)
    layer = double_layer(site_ket, pad)
    mixed = jnp.einsum("abm,ax->bmx", env_local, bond_mat, preferred_element_type=F32).astype(BF16)
    bond_term = jnp.einsum("bma,amc->bc", mixed, env_right, preferred_element_type=F32)
    bond_slots = lax.dynamic_update_slice(
        jnp.zeros((chi_all, chi_all), F32), bond_term, (lax.axis_index("chi") * rows, 0)
    )
    mid_all, bond_slots = lax.optimization_barrier((mid_all, bond_slots))
    bond_sum = lax.psum(bond_slots, ("chi", "dl"))
    right_cut = site_output(site_input(env_local, mid_all), layer, pad)
    center_term = jnp.einsum(
        "amdb,amc->bdc", right_cut[:, :, :leg_width], env_right, preferred_element_type=F32
    ).astype(BF16)
    iso_all, center_term, bond_sum = lax.optimization_barrier((iso_all, center_term, bond_sum))
    bond_full = bond_sum.astype(BF16)
    center_part = lax.psum_scatter(center_term, "dl", scatter_dimension=0, tiled=True)
    cross_part = jnp.einsum("bdc,bdy->cy", center_part, center_part, preferred_element_type=F32)

    def env_piece(cut):
        term = jnp.einsum(
            "cmdb,bdk->kmc", cut[:, :, :leg_width], bra_iso, preferred_element_type=F32
        ).astype(BF16)
        return lax.psum_scatter(term, "chi", scatter_dimension=0, tiled=True).astype(F32)

    half = leg_width // 2 * pad
    left_flat = site_input(env_local, iso_all)
    left_early = site_output(left_flat, layer[:, :half], pad)
    left_early, left_flat, cross_part, center_part = lax.optimization_barrier(
        (left_early, left_flat, cross_part, center_part)
    )
    cross = lax.psum(cross_part, ("chi", "dl"))
    center_all = lax.all_gather(center_part, "dl", axis=0, tiled=True)
    left_late = site_output(left_flat, layer[:, half:], pad)
    env_new = jnp.concatenate([env_piece(left_early), env_piece(left_late)], axis=1)
    bond_wide = bond_full.astype(F32)
    gram = jnp.dot(jnp.dot(bond_wide, cross, precision=HIGH), bond_wide.T, precision=HIGH)
    one = jnp.eye(chi_all, dtype=F32)
    norm_sum = jnp.sum(gram * one)
    factor = 0.25 * math.sqrt(chi_all) / jnp.sqrt(norm_sum)
    gram = gram * (factor * factor)
    product = None
    for sweep_index in range(ITERS):
        step = 1.5 * one - 0.5 * gram
        product = step if product is None else jnp.dot(product, step, precision=HIGH)
        if sweep_index < ITERS - 1:
            gram = jnp.dot(jnp.dot(step, gram, precision=HIGH), step, precision=HIGH)
    mine = lax.dynamic_slice_in_dim(product, lax.axis_index("dl") * col_count, col_count, 1)
    weight = lax.dot_general(bond_wide, mine, (((0,), (0,)), ((), ())), precision=HIGH)
    weight = weight * (factor * math.sqrt(chi_all * leg_width))
    new_left = jnp.einsum("bdc,cx->bdx", center_all.astype(F32), weight, precision=HIGH)
    return (env_new[None], new_left[None])


def solution(mesh):
    placed = (
        P("cell", None, "chi", None),
        P("cell", "chi", None, "dl"),
        P("cell", "chi", None, "dl"),
        P("cell", "dl", None, None),
        P("cell", None, "dl"),
        P("cell", None, None, None, None, None),
    )
    return jax.shard_map(
        shards,
        mesh=mesh,
        in_specs=placed,
        out_specs=(P("cell", "chi", None, "dl"), P("cell", "chi", None, "dl")),
        check_vma=False,
    )
```

profile of v0, /device:TPU:0, one launch (start us, length us, event | category | flops | bytes accessed | tf_op | source)
XLA Modules:
  0.0 800.2 jit_solution(4183132327198189968)
XLA Ops:
  14.1 7.7 fusion.52
  21.8 11.0 %convolution_multiply_fusion.1 = f32[1440,1440]{1,0:T(8,128)} fusion(f32[1440,1440]{1,0:T(8,128)} %fusion.52, bf16[36,36]{1,0:T(8,128)(2,1)S(1)} %reshape_squeeze.6, s32[1440]{0:T(1024)S(1)} %get-tuple-element.30, s32[1440]{0:T(1024)S(1)} %get-tuple-element.33, s32[1440]{0:T(1024)S(1)} %get-tuple-element.31, s32[1440]{0:T(1024)S(1)} %get-tuple-element.32, ...), kind=kOutput, calls=%fused_computation.13 | convolution fusion | flops 157127040 | bytes 16617312 | tf_op jit(solution)/shard_map/dot_general | solution.py:55
  33.0 7.3 fusion.53
  40.3 12.5 %fusion.7 = bf16[1440,1440]{1,0:T(8,128)(2,1)} fusion(f32[1440,1440]{1,0:T(8,128)} %convolution_multiply_fusion.1, f32[1440,1440]{1,0:T(8,128)} %fusion.53, bf16[36,36]{1,0:T(8,128)(2,1)S(1)} %reshape_squeeze.7, s32[1440]{0:T(1024)S(1)} %get-tuple-element.30, s32[1440]{0:T(1024)S(1)} %get-tuple-element.33, s32[1440]{0:T(1024)S(1)} %get-tuple-element.31, ...), kind=kOutput, calls=%fused_computation.15 | convolution fusion | flops 161274240 | bytes 20764512 | tf_op jit(solution)/shard_map/dot_general | solution.py:55
  52.9 6.5 fusion.49
  59.5 15.4 %all-gather.7.cloned.1.call-done = bf16[128,40,512]{2,1,0:T(8,128)(2,1)} async-done(((bf16[128,40,128]{2,1,0:T(8,128)(2,1)}), bf16[128,40,512]{2,1,0:T(8,128)(2,1)}) %all-gather.7.cloned.1.call-update) | async-done | bytes 5242896 | tf_op jit(solution)/shard_map/all_gather | solution.py:80
  74.8 32.4 %convolution_convert_fusion.2 = bf16[128,40,128,36]{2,1,3,0:T(8,128)(2,1)} fusion(bf16[128,40,512]{2,1,0:T(8,128)(2,1)} %all-gather.7.cloned.1.call-done, bf16[1,512,128,36]{2,1,3,0:T(8,128)(2,1)} %param.6), kind=kOutput, calls=%fused_computation.4 | convolution fusion | flops 24182784000 | bytes 57147392 | tf_op jit(solution)/shard_map/abm,csa->cmsb/dot_general | solution.py:67
  107.2 98.4 %all-reduce.6 = bf16[512,512]{1,0:T(8,128)(2,1)} all-reduce(f32[512,512]{1,0:T(8,128)S(1)} %fusion.49), channel_id=1, replica_groups=mesh['chi'=4,'dl'=4,'cell'=2] {'chi','dl'}, use_global_device_ids=true, to_apply=%region_0.1 | all-reduce | flops 262144 | bytes 1572864 | tf_op jit(solution)/shard_map/psum | solution.py:106
  205.6 81.7 %convolution_convert_fusion = bf16[128,128,1440]{1,2,0:T(8,128)(2,1)} fusion(bf16[128,1440,128]{2,1,0:T(8,128)(2,1)} %bitcast.157, bf16[1440,1440]{1,0:T(8,128)(2,1)} %fusion.7), kind=kOutput, calls=%fused_computation.2 | convolution fusion | flops 67971317760 | bytes 98519040 | tf_op jit(solution)/shard_map/tn,ctb->cnb/dot_general | solution.py:74
  287.3 37.6 %fusion.10 = bf16[128,36,512]{2,0,1:T(8,128)(2,1)} fusion(bf16[1,128,36,512]{3,1,2,0:T(8,128)(2,1)S(1)} %copy-done.7, bf16[128,36,36,128]{3,2,1,0:T(8,128)(2,1)} %bitcast.158), kind=kOutput, calls=%fused_computation.18 | convolution fusion | flops 21745631232 | bytes 51904512 | tf_op jit(solution)/shard_map/amdb,amc->bdc/dot_general | solution.py:108
  326.2 2.8 collective-permute-done
  330.1 32.4 %convolution_convert_fusion.1 = bf16[128,40,128,36]{2,1,3,0:T(8,128)(2,1)} fusion(bf16[128,40,512]{2,1,0:T(8,128)(2,1)} %all-gather.5.cloned.1.call-done, bf16[1,512,128,36]{2,1,3,0:T(8,128)(2,1)} %param.6), kind=kOutput, calls=%fused_computation.3 | convolution fusion | flops 24182784000 | bytes 57147392 | tf_op jit(solution)/shard_map/abm,csa->cmsb/dot_general | solution.py:67
  362.5 45.4 %convolution_convert_fusion.4 = bf16[128,128,720]{1,2,0:T(8,128)(2,1)} fusion(bf16[128,1440,128]{2,1,0:T(8,128)(2,1)} %bitcast.155, bf16[1440,1440]{1,0:T(8,128)(2,1)} %fusion.7), kind=kOutput, calls=%fused_computation.10 | convolution fusion | flops 33985658880 | bytes 72990720 | tf_op jit(solution)/shard_map/tn,ctb->cnb/dot_general | solution.py:74
  408.0 3.6 convolution_bitcast_fusion.1
  411.6 46.5 %convolution_convert_fusion.3 = bf16[128,128,720]{1,2,0:T(8,128)(2,1)} fusion(bf16[128,1440,128]{2,1,0:T(8,128)(2,1)} %bitcast.156, bf16[1440,1440]{1,0:T(8,128)(2,1)} %fusion.7), kind=kOutput, calls=%fused_computation.9 | convolution fusion | flops 33985658880 | bytes 72990720 | tf_op jit(solution)/shard_map/tn,ctb->cnb/dot_general | solution.py:74
  458.2 41.3 %all-gather.9.cloned.1.call-done = bf16[128,36,512]{2,0,1:T(8,128)(2,1)} async-done(((bf16[128,36,128]{2,0,1:T(8,128)(2,1)}), bf16[128,36,512]{2,0,1:T(8,128)(2,1)}) %all-gather.9.cloned.1.call-update) | async-done | bytes 4718608 | tf_op jit(solution)/shard_map/all_gather | solution.py:98
  499.4 15.8 %bitcast_convert_fusion.1 = bf16[128,18,512]{2,0,1:T(8,128)(2,1)S(1)} fusion(bf16[128,36,512]{2,0,1:T(8,128)(2,1)} %all-gather.9.cloned.1.call-done, bf16[128,18,36,128]{3,2,1,0:T(8,128)(2,1)} %bitcast.160), kind=kOutput, calls=%fused_computation.19 | convolution fusion | flops 10872815616 | bytes 28311552 | tf_op jit(solution)/shard_map/cmdb,bdk->kmc/dot_general | solution.py:117
  515.2 2.4 copy.82
  517.7 15.8 %bitcast_convert_fusion.2 = bf16[128,18,512]{2,0,1:T(8,128)(2,1)S(1)} fusion(bf16[128,36,512]{2,0,1:T(8,128)(2,1)} %all-gather.9.cloned.1.call-done, bf16[128,18,40,128]{3,2,1,0:T(8,128)(2,1)} %bitcast.159), kind=kOutput, calls=%fused_computation.20 | convolution fusion | flops 10872815616 | bytes 30670848 | tf_op jit(solution)/shard_map/cmdb,bdk->kmc/dot_general | solution.py:117
  536.8 77.7 %all-reduce.5.cloned.1.call-done = f32[512,512]{1,0:T(8,128)} async-done(((f32[512,512]{1,0:T(8,128)}), f32[512,512]{1,0:T(8,128)}) %all-reduce.5.cloned.1.call-update) | async-done | bytes 1048592 | tf_op jit(solution)/shard_map/psum | solution.py:128
  631.8 22.7 %reduce-scatter.12.cloned.1.call-done = bf16[128,2304]{1,0:T(8,128)(2,1)} async-done(((bf16[512,2304]{1,0:T(8,128)(2,1)}), bf16[128,2304]{1,0:T(8,128)(2,1)}) %reduce-scatter.12.cloned.1.call-update) | async-done | bytes 589840
  655.8 39.7 %reduce-scatter.10.cloned.1.call-done = bf16[128,2304]{1,0:T(8,128)(2,1)} async-done(((bf16[512,2304]{1,0:T(8,128)(2,1)}), bf16[128,2304]{1,0:T(8,128)(2,1)}) %reduce-scatter.10.cloned.1.call-update) | async-done | bytes 589840
  700.8 85.7 %all-gather.11.cloned.1.call-done = bf16[128,36,512]{2,0,1:T(8,128)(2,1)} async-done(((bf16[32,36,512]{2,0,1:T(8,128)(2,1)}), bf16[128,36,512]{2,0,1:T(8,128)(2,1)}) %all-gather.11.cloned.1.call-update) | async-done | bytes 4718608 | tf_op jit(solution)/shard_map/all_gather | solution.py:129
  786.5 6.3 convolution_bitcast_fusion
  (66 shorter events, 35.9 us)
Async XLA Ops:
  7.2 45.8 %copy-start = (bf16[1,512,128]{2,1,0:T(8,128)(2,1)S(1)}, bf16[1,512,128]{2,1,0:T(8,128)(2,1)}, u32[]{:S(2)}) copy-start(bf16[1,512,128]{2,1,0:T(8,128)(2,1)} %param.10) | copy-start | bytes 393220
  7.2 3.6 copy-start.3
  7.2 67.6 %all-gather.7.cloned.1.call-start = ((), (), s32[]{:S(2)}) async-start(), calls=%async_computation.4 | async-start | bytes 6553600 | tf_op jit(solution)/shard_map/all_gather | solution.py:80
  9.5 3.9 copy-start.6
  10.7 314.2 %all-gather.5.cloned.1.call-start = ((), (), s32[]{:S(2)}) async-start(), calls=%async_computation.3 | async-start | bytes 6553600 | tf_op jit(solution)/shard_map/all_gather | solution.py:80
  13.3 394.7 %reduce-scatter.8.cloned.1.call-start = ((), (), s32[]{:S(2)}) async-start(), calls=%async_computation.5 | async-start | bytes 5898240 | tf_op jit(solution)/shard_map/reduce_scatter | solution.py:113
  205.6 81.7 %copy-start.7 = (bf16[1,128,36,512]{3,1,2,0:T(8,128)(2,1)S(1)}, bf16[1,128,36,512]{3,1,2,0:T(8,128)(2,1)}, u32[]{:S(2)}) copy-start(bf16[1,128,36,512]{3,1,2,0:T(8,128)(2,1)} %param.9) | copy-start | bytes 14155780
  324.9 1.3 copy-start.4
  324.9 174.5 %all-gather.9.cloned.1.call-start = ((), (), s32[]{:S(2)}) async-start(), calls=%async_computation.6 | async-start | bytes 5898240 | tf_op jit(solution)/shard_map/all_gather | solution.py:98
  326.2 2.8 collective-permute-start
  329.0 1.0 copy-start.5
  330.1 284.4 %all-reduce.5.cloned.1.call-start = ((), (), s32[]{:S(2)}) async-start(), calls=%async_computation.8 | async-start | bytes 2097152 | tf_op jit(solution)/shard_map/psum | solution.py:128
  458.1 196.4 %reduce-scatter.12.cloned.1.call-start = ((), (), s32[]{:S(2)}) async-start(), calls=%async_computation.10 | async-start | bytes 2949120
  517.6 177.9 %reduce-scatter.10.cloned.1.call-start = ((), (), s32[]{:S(2)}) async-start(), calls=%async_computation.9 | async-start | bytes 2949120
  533.5 81.0 %copy-start.2 = (bf16[512,512]{1,0:T(8,128)(2,1)S(1)}, bf16[512,512]{1,0:T(8,128)(2,1)}, u32[]{:S(2)}) copy-start(bf16[512,512]{1,0:T(8,128)(2,1)} %all-reduce.6) | copy-start | bytes 1572868
  536.0 250.5 %all-gather.11.cloned.1.call-start = ((), (), s32[]{:S(2)}) async-start(), calls=%async_computation.7 | async-start | bytes 5898240 | tf_op jit(solution)/shard_map/all_gather | solution.py:129
  698.9 94.0 %copy-start.1 = (bf16[1,512,128]{2,1,0:T(8,128)(2,1)S(1)}, bf16[1,512,128]{2,1,0:T(8,128)(2,1)}, u32[]{:S(2)}) copy-start(bf16[1,512,128]{2,1,0:T(8,128)(2,1)} %param.10) | copy-start | bytes 393220
Sparse Core Ops, SparseCore 0:
  10.8 63.9 all-gather.6
  77.2 69.7 all-gather.4
  325.1 82.6 reduce-scatter.7
  409.7 89.6 all-gather.8
  504.6 109.8 all-reduce.4
  618.0 36.4 reduce-scatter.11
  658.1 37.3 reduce-scatter.9
  697.1 89.3 all-gather.10
where the time goes:
time: 810 us; the launch traced here: 800 us
  matrix products  379 us (47%)
  waiting for transfers between devices  286 us (35%)
  blocking collectives  98.4 us (12%)
  local copies, waits for them, and re-layouts  19.4 us (2%)
  between operations  15.5 us (2%)
    dot_general x3, matrix products, site_output(): jnp.einsum('tn,ctb->cnb', layer, flat, preferred_element_type=F32)  174 us
    psum x1, blocking collectives, shards(): bond_sum = lax.psum(bond_slots, ('chi', 'dl'))  98.4 us
    all_gather x1, waiting for transfers between devices, shards(): center_all = lax.all_gather(center_part, 'dl', axis=0, tiled=True)  85.7 us
    psum x1, waiting for transfers between devices, shards(): cross = lax.psum(cross_part, ('chi', 'dl'))  77.7 us
    dot_general x2, matrix products, site_input(): jnp.einsum('abm,csa->cmsb', env, stacked, preferred_element_type=F32)  64.8 us
    unnamed x10, waiting for transfers between devices  63 us
    all_gather x1, waiting for transfers between devices, shards(): bra_iso = lax.all_gather(next_iso, 'dl', axis=2, tiled=True)  41.3 us
    dot_general x1, matrix products, shards(): jnp.einsum('amdb,amc->bdc', right_cut[:, :, :leg_width], env_right, prefe...  37.6 us
  transfers between devices with their start and end apart: 9, of which 7 were waited for; matrix products, arithmetic and copies ran while one was open for 48% of the time, Pallas kernels for 0%

commit v1 on v0

--- a/solution.py
+++ b/solution.py
@@ -126,7 +126,22 @@
         (left_early, left_flat, cross_part, center_part)
     )
     cross = lax.psum(cross_part, ("chi", "dl"))
-    center_all = lax.all_gather(center_part, "dl", axis=0, tiled=True)
+    ways, here, k = (lax.axis_size("dl"), lax.axis_index("dl"), center_part.shape[0])
+    dims = [n_2 * ways if d == 0 else n_2 for d, n_2 in enumerate(center_part.shape)]
+    center_all = lax.dynamic_update_slice_in_dim(
+        jnp.zeros(dims, center_part.dtype), center_part, here * k, axis=0
+    )
+    going_up = going_down = center_part
+    for far in range(1, ways // 2 + 1):
+        going_up = lax.ppermute(going_up, "dl", [(d, (d + 1) % ways) for d in range(ways)])
+        center_all = lax.dynamic_update_slice_in_dim(
+            center_all, going_up, (here - far) % ways * k, axis=0
+        )
+        if 2 * far < ways:
+            going_down = lax.ppermute(going_down, "dl", [(d, (d - 1) % ways) for d in range(ways)])
+            center_all = lax.dynamic_update_slice_in_dim(
+                center_all, going_down, (here + far) % ways * k, axis=0
+            )
     left_late = site_output(left_flat, layer[:, half:], pad)
     env_new = jnp.concatenate([env_piece(left_early), env_piece(left_late)], axis=1)
     bond_wide = bond_full.astype(F32)

time: 810 us -> 763 us (0.942)
  waiting for transfers between devices: 286 us -> 219 us
  local copies, waits for them, and re-layouts: 19.4 us -> 32.3 us
    all_gather x1 -> x0, waiting for transfers between devices: 85.7 us -> none  [shards(): center_all = lax.all_gather(center_part, 'dl', axis=0, tiled=True)]
    all_gather x1, waiting for transfers between devices: 41.3 us -> 79.9 us  [shards(): bra_iso = lax.all_gather(next_iso, 'dl', axis=2, tiled=True)]
    unnamed x10 -> x9, waiting for transfers between devices: 63 us -> 27 us
    ppermute x0 -> x3, waiting for transfers between devices: none -> 18.4 us  [the longest x2 18.4 us: shards(): lax.ppermute(going_up, 'dl', [(d, (d + 1) % ways) for d in range(ways)])]
    dynamic_update_slice x0 -> x4, local copies, waits for them, and re-layouts: none -> 9.9 us  [the longest x2 4.94 us: shards(): lax.dynamic_update_slice_in_dim(center_all, going_up, (here - far) % ways...]
  transfers between devices with their start and end apart: 9 -> 11, of which waited for: 7 -> 6; matrix products, arithmetic and copies ran while one was open for 48% -> 54% of each run, Pallas kernels for 0% -> 0%
where the time goes in v1:
time: 763 us; the launch traced here: 753 us
  matrix products  382 us (50%)
  waiting for transfers between devices  219 us (29%)
  blocking collectives  98.4 us (13%)
  local copies, waits for them, and re-layouts  32.3 us (4%)
  between operations  15.5 us (2%)
    dot_general x3, matrix products, site_output(): jnp.einsum('tn,ctb->cnb', layer, flat, preferred_element_type=F32)  174 us
    psum x1, blocking collectives, shards(): bond_sum = lax.psum(bond_slots, ('chi', 'dl'))  98.4 us
    all_gather x1, waiting for transfers between devices, shards(): bra_iso = lax.all_gather(next_iso, 'dl', axis=2, tiled=True)  79.9 us
    psum x1, waiting for transfers between devices, shards(): cross = lax.psum(cross_part, ('chi', 'dl'))  75.2 us
    dot_general x2, matrix products, site_input(): jnp.einsum('abm,csa->cmsb', env, stacked, preferred_element_type=F32)  64.8 us
    dot_general x1, matrix products, shards(): jnp.einsum('amdb,amc->bdc', right_cut[:, :, :leg_width], env_right, prefe...  37.6 us
    dot_general x2, matrix products, env_piece(): jnp.einsum('cmdb,bdk->kmc', cut[:, :, :leg_width], bra_iso, preferred_ele...  31.8 us
    unnamed x9, waiting for transfers between devices  27 us
  transfers between devices with their start and end apart: 11, of which 6 were waited for; matrix products, arithmetic and copies ran while one was open for 54% of the time, Pallas kernels for 0%

profile of v1, /device:TPU:0, one launch (start us, length us, event | category | flops | bytes accessed | tf_op | source)
XLA Modules:
  0.0 753.4 jit_solution(3187734358916737527)
XLA Ops:
  14.1 7.7 %fusion.52 = f32[1440,1440]{1,0:T(8,128)} fusion(bf16[36,36]{1,0:T(8,128)(2,1)S(1)} %reshape_squeeze.6, s32[1440]{0:T(1024)S(1)} %get-tuple-element.30, s32[1440]{0:T(1024)S(1)} %get-tuple-element.33, s32[1440]{0:T(1024)S(1)} %get-tuple-element.31, s32[1440]{0:T(1024)S(1)} %get-tuple-element.32, pred[1440]{0:T(1024)(128)(4,1)S(1)} %get-tuple-element.34, ...), kind=kOutput, calls=%fused_computation.67 | convolution fusion | flops 155468160 | bytes 8322912 | tf_op jit(solution)/shard_map/dot_general | solution.py:52
  21.8 11.0 %convolution_multiply_fusion.1 = f32[1440,1440]{1,0:T(8,128)} fusion(f32[1440,1440]{1,0:T(8,128)} %fusion.52, bf16[36,36]{1,0:T(8,128)(2,1)S(1)} %reshape_squeeze.6, s32[1440]{0:T(1024)S(1)} %get-tuple-element.30, s32[1440]{0:T(1024)S(1)} %get-tuple-element.33, s32[1440]{0:T(1024)S(1)} %get-tuple-element.31, s32[1440]{0:T(1024)S(1)} %get-tuple-element.32, ...), kind=kOutput, calls=%fused_computation.13 | convolution fusion | flops 157127040 | bytes 16617312 | tf_op jit(solution)/shard_map/dot_general | solution.py:55
  33.0 7.3 fusion.53
  40.3 12.5 %fusion.7 = bf16[1440,1440]{1,0:T(8,128)(2,1)} fusion(f32[1440,1440]{1,0:T(8,128)} %convolution_multiply_fusion.1, f32[1440,1440]{1,0:T(8,128)} %fusion.53, bf16[36,36]{1,0:T(8,128)(2,1)S(1)} %reshape_squeeze.7, s32[1440]{0:T(1024)S(1)} %get-tuple-element.30, s32[1440]{0:T(1024)S(1)} %get-tuple-element.33, s32[1440]{0:T(1024)S(1)} %get-tuple-element.31, ...), kind=kOutput, calls=%fused_computation.15 | convolution fusion | flops 161274240 | bytes 20764512 | tf_op jit(solution)/shard_map/dot_general | solution.py:55
  52.9 6.5 fusion.49
  59.5 15.4 %all-gather.6.cloned.1.call-done = bf16[128,40,512]{2,1,0:T(8,128)(2,1)} async-done(((bf16[128,40,128]{2,1,0:T(8,128)(2,1)}), bf16[128,40,512]{2,1,0:T(8,128)(2,1)}) %all-gather.6.cloned.1.call-update) | async-done | bytes 5242896 | tf_op jit(solution)/shard_map/all_gather | solution.py:80
  74.8 32.4 %convolution_convert_fusion.2 = bf16[128,40,128,36]{2,1,3,0:T(8,128)(2,1)} fusion(bf16[128,40,512]{2,1,0:T(8,128)(2,1)} %all-gather.6.cloned.1.call-done, bf16[1,512,128,36]{2,1,3,0:T(8,128)(2,1)} %param.6), kind=kOutput, calls=%fused_computation.4 | convolution fusion | flops 24182784000 | bytes 57147392 | tf_op jit(solution)/shard_map/abm,csa->cmsb/dot_general | solution.py:67
  107.2 98.4 %all-reduce.6 = bf16[512,512]{1,0:T(8,128)(2,1)} all-reduce(f32[512,512]{1,0:T(8,128)S(1)} %fusion.49), channel_id=1, replica_groups=mesh['chi'=4,'dl'=4,'cell'=2] {'chi','dl'}, use_global_device_ids=true, to_apply=%region_0.1 | all-reduce | flops 262144 | bytes 1572864 | tf_op jit(solution)/shard_map/psum | solution.py:106
  205.6 81.7 %convolution_convert_fusion = bf16[128,128,1440]{1,2,0:T(8,128)(2,1)} fusion(bf16[128,1440,128]{2,1,0:T(8,128)(2,1)} %bitcast.157, bf16[1440,1440]{1,0:T(8,128)(2,1)} %fusion.7), kind=kOutput, calls=%fused_computation.2 | convolution fusion | flops 67971317760 | bytes 98519040 | tf_op jit(solution)/shard_map/tn,ctb->cnb/dot_general | solution.py:74
  287.3 37.6 %fusion.10 = bf16[128,36,512]{2,0,1:T(8,128)(2,1)} fusion(bf16[1,128,36,512]{3,1,2,0:T(8,128)(2,1)S(1)} %copy-done.7, bf16[128,36,36,128]{3,2,1,0:T(8,128)(2,1)} %bitcast.158), kind=kOutput, calls=%fused_computation.18 | convolution fusion | flops 21745631232 | bytes 51904512 | tf_op jit(solution)/shard_map/amdb,amc->bdc/dot_general | solution.py:108
  326.2 2.8 collective-permute-done
  330.1 32.4 %convolution_convert_fusion.1 = bf16[128,40,128,36]{2,1,3,0:T(8,128)(2,1)} fusion(bf16[128,40,512]{2,1,0:T(8,128)(2,1)} %all-gather.4.cloned.1.call-done, bf16[1,512,128,36]{2,1,3,0:T(8,128)(2,1)} %param.6), kind=kOutput, calls=%fused_computation.3 | convolution fusion | flops 24182784000 | bytes 57147392 | tf_op jit(solution)/shard_map/abm,csa->cmsb/dot_general | solution.py:67
  362.5 45.2 %convolution_convert_fusion.4 = bf16[128,128,720]{1,2,0:T(8,128)(2,1)} fusion(bf16[128,1440,128]{2,1,0:T(8,128)(2,1)} %bitcast.155, bf16[1440,1440]{1,0:T(8,128)(2,1)} %fusion.7), kind=kOutput, calls=%fused_computation.10 | convolution fusion | flops 33985658880 | bytes 72990720 | tf_op jit(solution)/shard_map/tn,ctb->cnb/dot_general | solution.py:74
  407.7 3.6 convolution_bitcast_fusion.1
  415.2 47.6 %convolution_convert_fusion.3 = bf16[128,128,720]{1,2,0:T(8,128)(2,1)} fusion(bf16[128,1440,128]{2,1,0:T(8,128)(2,1)} %bitcast.156, bf16[1440,1440]{1,0:T(8,128)(2,1)} %fusion.7), kind=kOutput, calls=%fused_computation.9 | convolution fusion | flops 33985658880 | bytes 72990720 | tf_op jit(solution)/shard_map/tn,ctb->cnb/dot_general | solution.py:74
  462.9 79.9 %all-gather.8.cloned.1.call-done = bf16[128,36,512]{2,0,1:T(8,128)(2,1)} async-done(((bf16[128,36,128]{2,0,1:T(8,128)(2,1)}), bf16[128,36,512]{2,0,1:T(8,128)(2,1)}) %all-gather.8.cloned.1.call-update) | async-done | bytes 4718608 | tf_op jit(solution)/shard_map/all_gather | solution.py:98
  542.8 15.9 %bitcast_convert_fusion.1 = bf16[128,18,512]{2,0,1:T(8,128)(2,1)S(1)} fusion(bf16[128,36,512]{2,0,1:T(8,128)(2,1)} %all-gather.8.cloned.1.call-done, bf16[128,18,36,128]{3,2,1,0:T(8,128)(2,1)} %bitcast.160), kind=kOutput, calls=%fused_computation.19 | convolution fusion | flops 10872815616 | bytes 28311552 | tf_op jit(solution)/shard_map/cmdb,bdk->kmc/dot_general | solution.py:117
  561.2 15.9 %bitcast_convert_fusion.2 = bf16[128,18,512]{2,0,1:T(8,128)(2,1)S(1)} fusion(bf16[128,36,512]{2,0,1:T(8,128)(2,1)} %all-gather.8.cloned.1.call-done, bf16[128,18,40,128]{3,2,1,0:T(8,128)(2,1)} %bitcast.159), kind=kOutput, calls=%fused_computation.20 | convolution fusion | flops 10872815616 | bytes 30670848 | tf_op jit(solution)/shard_map/cmdb,bdk->kmc/dot_general | solution.py:117
  577.1 2.8 copy.80
  579.9 2.7 broadcast_in_dim.21
  585.1 75.2 %all-reduce.5.cloned.1.call-done = f32[512,512]{1,0:T(8,128)} async-done(((f32[512,512]{1,0:T(8,128)}), f32[512,512]{1,0:T(8,128)}) %all-reduce.5.cloned.1.call-update) | async-done | bytes 1048592 | tf_op jit(solution)/shard_map/psum | solution.py:128
  685.3 18.4 %collective-permute-done.3 = bf16[32,36,512]{2,0,1:T(8,128)(2,1)} collective-permute-done((bf16[32,36,512]{2,0,1:T(8,128)(2,1)}, bf16[32,36,512]{2,0,1:T(8,128)(2,1)}, u32[]{:S(2)}, u32[]{:S(2)}) %collective-permute-start.3) | collective-permute-done | bytes 1179680 | tf_op jit(solution)/shard_map/ppermute | solution.py:136
  706.2 6.4 convolution_bitcast_fusion
  713.9 26.9 %reduce-scatter.10.cloned.1.call-done = bf16[128,2304]{1,0:T(8,128)(2,1)} async-done(((bf16[512,2304]{1,0:T(8,128)(2,1)}), bf16[128,2304]{1,0:T(8,128)(2,1)}) %reduce-scatter.10.cloned.1.call-update) | async-done | bytes 589840
  (74 shorter events, 51.6 us)
Async XLA Ops:
  7.2 45.8 %copy-start = (bf16[1,512,128]{2,1,0:T(8,128)(2,1)S(1)}, bf16[1,512,128]{2,1,0:T(8,128)(2,1)}, u32[]{:S(2)}) copy-start(bf16[1,512,128]{2,1,0:T(8,128)(2,1)} %param.10) | copy-start | bytes 393220
  7.2 3.6 copy-start.3
  7.2 67.6 %all-gather.6.cloned.1.call-start = ((), (), s32[]{:S(2)}) async-start(), calls=%async_computation.4 | async-start | bytes 6553600 | tf_op jit(solution)/shard_map/all_gather | solution.py:80
  9.5 3.9 copy-start.6
  10.7 314.2 %all-gather.4.cloned.1.call-start = ((), (), s32[]{:S(2)}) async-start(), calls=%async_computation.3 | async-start | bytes 6553600 | tf_op jit(solution)/shard_map/all_gather | solution.py:80
  13.3 394.5 %reduce-scatter.8.cloned.1.call-start = ((), (), s32[]{:S(2)}) async-start(), calls=%async_computation.5 | async-start | bytes 5898240 | tf_op jit(solution)/shard_map/reduce_scatter | solution.py:113
  205.6 81.7 %copy-start.7 = (bf16[1,128,36,512]{3,1,2,0:T(8,128)(2,1)S(1)}, bf16[1,128,36,512]{3,1,2,0:T(8,128)(2,1)}, u32[]{:S(2)}) copy-start(bf16[1,128,36,512]{3,1,2,0:T(8,128)(2,1)} %param.9) | copy-start | bytes 14155780
  324.9 1.3 copy-start.4
  324.9 217.9 %all-gather.8.cloned.1.call-start = ((), (), s32[]{:S(2)}) async-start(), calls=%async_computation.6 | async-start | bytes 5898240 | tf_op jit(solution)/shard_map/all_gather | solution.py:98
  326.2 2.8 collective-permute-start
  329.0 1.0 copy-start.5
  330.0 330.3 %all-reduce.5.cloned.1.call-start = ((), (), s32[]{:S(2)}) async-start(), calls=%async_computation.7 | async-start | bytes 2097152 | tf_op jit(solution)/shard_map/psum | solution.py:128
  411.4 263.4 %collective-permute-start.1 = (bf16[32,36,512]{2,0,1:T(8,128)(2,1)}, bf16[32,36,512]{2,0,1:T(8,128)(2,1)}, u32[]{:S(2)}, u32[]{:S(2)}) collective-permute-start(bf16[32,36,512]{2,0,1:T(8,128)(2,1)} %reduce-scatter.8.cloned.1.call-done), channel_id=1, source_target_pairs={{0,2},{2,4},{4,6},{6,0},{1,3},{3,5},{5,7},{7,1},{8,10},{10,12},{12... | collective-permute-start | bytes 3538952 | tf_op jit(solution)/shard_map/ppermute | solution.py:136
  412.8 270.1 %collective-permute-start.2 = (bf16[32,36,512]{2,0,1:T(8,128)(2,1)}, bf16[32,36,512]{2,0,1:T(8,128)(2,1)}, u32[]{:S(2)}, u32[]{:S(2)}) collective-permute-start(bf16[32,36,512]{2,0,1:T(8,128)(2,1)} %reduce-scatter.8.cloned.1.call-done), channel_id=1, source_target_pairs={{0,6},{2,0},{4,2},{6,4},{1,7},{3,1},{5,3},{7,5},{8,14},{10,8},{12,... | collective-permute-start | bytes 3538952 | tf_op jit(solution)/shard_map/ppermute | solution.py:141
  462.8 249.7 %reduce-scatter.12.cloned.1.call-start = ((), (), s32[]{:S(2)}) async-start(), calls=%async_computation.9 | async-start | bytes 2949120
  561.2 179.6 %reduce-scatter.10.cloned.1.call-start = ((), (), s32[]{:S(2)}) async-start(), calls=%async_computation.8 | async-start | bytes 2949120
  579.9 80.4 %copy-start.2 = (bf16[512,512]{1,0:T(8,128)(2,1)S(1)}, bf16[512,512]{1,0:T(8,128)(2,1)}, u32[]{:S(2)}) copy-start(bf16[512,512]{1,0:T(8,128)(2,1)} %all-reduce.6) | copy-start | bytes 1572868
  674.7 29.0 %collective-permute-start.3 = (bf16[32,36,512]{2,0,1:T(8,128)(2,1)}, bf16[32,36,512]{2,0,1:T(8,128)(2,1)}, u32[]{:S(2)}, u32[]{:S(2)}) collective-permute-start(bf16[32,36,512]{2,0,1:T(8,128)(2,1)} %collective-permute-done.1), channel_id=1, source_target_pairs={{0,2},{2,4},{4,6},{6,0},{1,3},{3,5},{5,7},{7,1},{8,10},{10,12},{12... | collective-permute-start | bytes 3538952 | tf_op jit(solution)/shard_map/ppermute | solution.py:136
  712.5 33.6 %copy-start.1 = (bf16[1,512,128]{2,1,0:T(8,128)(2,1)S(1)}, bf16[1,512,128]{2,1,0:T(8,128)(2,1)}, u32[]{:S(2)}) copy-start(bf16[1,512,128]{2,1,0:T(8,128)(2,1)} %param.10) | copy-start | bytes 393220
Sparse Core Ops, SparseCore 0:
  10.8 63.9 all-gather.5
  77.2 69.7 all-gather.3
  325.0 82.6 reduce-scatter.7
  409.7 133.0 all-gather.7
  547.9 112.3 all-reduce.4
  663.8 36.4 reduce-scatter.11
  703.4 37.3 reduce-scatter.9
